TPU v7x, 128 devices: a whole 4x4x4 slice. The times are simulated.
128 devices in a mesh: body: 2 (over y_lo), row: 8 (over y_hi, x), col: 8 (over z, core).
Axes of the slice: x: 4, y: 4 (y_hi: 2, y_lo: 2; y = y_hi * 2 + y_lo), z: 4, core: 2. Of those that a mesh axis runs over, the one named last changes fastest.
Arguments:
- lam_start: float32 [2, 128, 16384], P('body', None, ('row', 'col')), may hold values from -8 to 8
- load: float32 [2, 128, 16384], P('body', None, ('row', 'col')), may hold values from -24 to 24
- operator: bfloat16 [2, 16384, 8, 8, 256], P('body', 'row', None, 'col'), as said below
- partner: int32 [2, 16384], P('body', ('row', 'col')), may hold values from 0 to 16383, as said below
- active: int32 [16384], P(('row', 'col')), may hold values 0 or 1
- bounds: int32 [2, 2], P('body'), may hold values from 1 to 20, as said below
Outputs:
- multipliers: float32 [2, 128, 16384], P('body', None, ('row', 'col'))
- residual: float32 [2, 128, 16384], P('body', None, ('row', 'col'))
Inputs may be any that keep to these rules, and one draw needn't show every extreme that they name: Each operator F_b is symmetric, with positive diagonal. partner[0] maps every aligned block of 256 unknowns onto itself, one to one, and partner[1] is its inverse: partner[1, partner[0, i]] = i. bounds[b, 0] is 1 or 2 and bounds[b, 1] is 18 to 20.
All inputs are finite; a program needn't handle non-finite values. No bound on the sum of `active` on one device may be relied on, other than what follows from the above.
Results may differ from a plain program's by a relative error of at most 0.03.
The roundings to bfloat16 on the way count: a program that leaves them out, or rounds other values in their place, can miss the bound.
Values may be sent and summed in bfloat16 or wider, within the bound.
No kernel may reach another device: no remote copies, remote signals or barrier semaphores. Data moves between devices by JAX's collectives and lax.ppermute only.
A program may use at most 64 MiB of HBM per device.

v0:
```python
import jax
import jax.numpy as jnp
from jax import lax
from jax.sharding import PartitionSpec as P

K = 4


def swapped(value, axis, distance):
    mask = 2**distance
    pairs = [(source, source ^ mask) for source in range(lax.axis_size(axis))]
    return lax.ppermute(value, axis, pairs)


def clamp_local(lam, partner, active):
    peer = swapped(lam, "body", 0)
    width = lam.shape[1]
    local = partner % width
    mate = jnp.take(peer, local, axis=1)
    which = lax.axis_index("body")
    sign = (1 - 2 * which).astype(jnp.float32)
    flag_index = jnp.where(which == 0, jnp.arange(width, dtype=jnp.int32), local)
    flags = jnp.take(active, flag_index) > 0
    middle = 0.5 * (lam + mate)
    normal = 0.5 * sign * (lam - mate)
    normal = jnp.where(flags[None, :], jnp.maximum(normal, 0.0), normal)
    return middle + sign * normal


def apply_tile(field, tile):
    rounded = field.astype(jnp.bfloat16)
    partial_sum = lax.dot_general(
        lax.all_gather(rounded, "row", axis=1, tiled=True),
        tile,
        (((1,), (1,)), ((), ())),
        preferred_element_type=jnp.float32,
    )
    return lax.psum_scatter(partial_sum, "col", scatter_dimension=1, tiled=True)


def cheb_local(start, load, tile, lower, upper):
    theta = 0.5 * (upper + lower)
    delta = 0.5 * (upper - lower)
    sigma = theta / delta
    answer = start
    resid = load - apply_tile(answer, tile)
    direction = resid / theta
    rho = delta / theta
    for step in range(K):
        answer = answer + direction
        resid = resid - apply_tile(direction, tile)
        if step + 1 < K:
            rho_new = 1.0 / (2.0 * sigma - rho)
            direction = rho_new * rho * direction + 2.0 * rho_new / delta * resid
            rho = rho_new
    return (answer, resid)


def per_device(lam_start, load, operator, partner, active, bounds):
    tile = operator.reshape(operator.shape[1], operator.shape[2] * operator.shape[4])
    lower = bounds[0, 0].astype(jnp.float32)
    upper = bounds[0, 1].astype(jnp.float32)
    own_load = load[0]
    own_partner = partner[0]
    first = clamp_local(lam_start[0], own_partner, active)
    second, unused = cheb_local(first, own_load, tile, lower, upper)
    third = clamp_local(second, own_partner, active)
    answer, resid = cheb_local(third, own_load, tile, lower, upper)
    return (answer[None], resid[None])


def solution(mesh):
    return jax.shard_map(
        per_device,
        mesh=mesh,
        in_specs=(
            P("body", None, ("row", "col")),
            P("body", None, ("row", "col")),
            P("body", "row", None, "col", None),
            P("body", ("row", "col")),
            P(("row", "col")),
            P("body", None),
        ),
        out_specs=(P("body", None, ("row", "col")), P("body", None, ("row", "col"))),
        check_vma=False,
    )
```

profile of v0, /device:TPU:0, one launch (start us, length us, event | category | flops | bytes accessed | tf_op | source)
XLA Modules:
  0.0 709.3 jit_solution(16832281575850132127)
XLA Ops:
  7.2 0.0 reduce-scatter.10.cloned.1.call-start
  7.2 1.8 collective-permute-start
  9.0 0.7 compare_and_fusion
  9.7 1.9 gather_fusion.1
  11.7 10.3 %copy.16 = bf16[256,8,8,256]{3,1,2,0:T(8,128)(2,1)} copy(bf16[256,8,8,256]{3,2,1,0:T(8,128)(2,1)} %bitcast.89) | data formatting | bytes 16777216
  22.1 0.1 copy.12
  22.2 0.7 gather_fusion
  22.9 0.1 copy.13
  23.0 0.1 fusion.17
  23.1 35.3 %all_gather.27 = bf16[128,2048]{1,0:T(8,128)(2,1)S(1)} all-gather(bf16[128,256]{1,0:T(8,128)(2,1)S(1)} %fusion.17), channel_id=1, replica_groups=mesh['body'=2,'row'=8,'col'=8] {'row'}, dimensions={1}, use_global_device_ids=true | all-gather | bytes 589824 | tf_op jit(solution)/shard_map/all_gather | solution.py:33
  58.4 7.3 %fusion.24 = f32[128,2048]{1,0:T(8,128)} fusion(bf16[128,2048]{1,0:T(8,128)(2,1)S(1)} %all_gather.27, bf16[2048,2048]{1,0:T(8,128)(2,1)} %bitcast.80), kind=kOutput, calls=%fused_computation.52 | convolution fusion | flops 1073741824 | bytes 9961472 | tf_op jit(solution)/shard_map/dot_general | solution.py:32
  65.7 0.0 reduce-scatter.10.cloned.1.call-update
  65.7 0.0 reduce-scatter.12.cloned.1.call-start
  65.8 0.6 fusion.23
  67.7 32.2 %reduce-scatter.10.cloned.1.call-done = f32[128,256]{1,0:T(8,128)} async-done(((f32[128,2048]{1,0:T(8,128)}), f32[128,256]{1,0:T(8,128)}) %reduce-scatter.10.cloned.1.call-update) | async-done | bytes 131088 | tf_op jit(solution)/shard_map/reduce_scatter | solution.py:38
  99.9 1.0 fusion.22
  100.9 35.5 %all_gather.28 = bf16[128,2048]{1,0:T(8,128)(2,1)S(1)} all-gather(bf16[128,256]{1,0:T(8,128)(2,1)S(1)} %get-tuple-element.17), channel_id=1, replica_groups=mesh['body'=2,'row'=8,'col'=8] {'row'}, dimensions={1}, use_global_device_ids=true | all-gather | bytes 589824 | tf_op jit(solution)/shard_map/all_gather | solution.py:33
  136.3 7.4 %fusion.25 = f32[128,2048]{1,0:T(8,128)} fusion(bf16[128,2048]{1,0:T(8,128)(2,1)S(1)} %all_gather.28, bf16[2048,2048]{1,0:T(8,128)(2,1)} %bitcast.81), kind=kOutput, calls=%fused_computation.53 | convolution fusion | flops 1073741824 | bytes 9961472 | tf_op jit(solution)/shard_map/dot_general | solution.py:32
  143.7 0.0 reduce-scatter.14.cloned.1.call-start
  143.9 30.1 %reduce-scatter.12.cloned.1.call-done = f32[128,256]{1,0:T(8,128)} async-done(((f32[128,2048]{1,0:T(8,128)}), f32[128,256]{1,0:T(8,128)}) %reduce-scatter.12.cloned.1.call-update) | async-done | bytes 131088 | tf_op jit(solution)/shard_map/reduce_scatter | solution.py:38
  174.1 1.0 fusion.12
  175.0 35.7 %all_gather.29 = bf16[128,2048]{1,0:T(8,128)(2,1)S(1)} all-gather(bf16[128,256]{1,0:T(8,128)(2,1)S(1)} %get-tuple-element.15), channel_id=1, replica_groups=mesh['body'=2,'row'=8,'col'=8] {'row'}, dimensions={1}, use_global_device_ids=true | all-gather | bytes 589824 | tf_op jit(solution)/shard_map/all_gather | solution.py:33
  210.7 7.3 %fusion.26 = f32[128,2048]{1,0:T(8,128)} fusion(bf16[128,2048]{1,0:T(8,128)(2,1)S(1)} %all_gather.29, bf16[2048,2048]{1,0:T(8,128)(2,1)} %bitcast.82), kind=kOutput, calls=%fused_computation.54 | convolution fusion | flops 1073741824 | bytes 9961472 | tf_op jit(solution)/shard_map/dot_general | solution.py:32
  218.1 0.0 reduce-scatter.14.cloned.1.call-update
  218.1 0.0 reduce-scatter.16.cloned.1.call-start
  218.2 30.2 %reduce-scatter.14.cloned.1.call-done = f32[128,256]{1,0:T(8,128)} async-done(((f32[128,2048]{1,0:T(8,128)}), f32[128,256]{1,0:T(8,128)}) %reduce-scatter.14.cloned.1.call-update) | async-done | bytes 131088 | tf_op jit(solution)/shard_map/reduce_scatter | solution.py:38
  248.5 1.0 fusion.8
  249.4 35.5 %all_gather.30 = bf16[128,2048]{1,0:T(8,128)(2,1)S(1)} all-gather(bf16[128,256]{1,0:T(8,128)(2,1)S(1)} %get-tuple-element.13), channel_id=1, replica_groups=mesh['body'=2,'row'=8,'col'=8] {'row'}, dimensions={1}, use_global_device_ids=true | all-gather | bytes 589824 | tf_op jit(solution)/shard_map/all_gather | solution.py:33
  284.9 7.4 %fusion.27 = f32[128,2048]{1,0:T(8,128)} fusion(bf16[128,2048]{1,0:T(8,128)(2,1)S(1)} %all_gather.30, bf16[2048,2048]{1,0:T(8,128)(2,1)} %bitcast.83), kind=kOutput, calls=%fused_computation.55 | convolution fusion | flops 1073741824 | bytes 9961472 | tf_op jit(solution)/shard_map/dot_general | solution.py:32
  292.3 0.0 reduce-scatter.16.cloned.1.call-update
  292.3 0.0 reduce-scatter.18.cloned.1.call-start
  292.4 30.2 %reduce-scatter.16.cloned.1.call-done = f32[128,256]{1,0:T(8,128)} async-done(((f32[128,2048]{1,0:T(8,128)}), f32[128,256]{1,0:T(8,128)}) %reduce-scatter.16.cloned.1.call-update) | async-done | bytes 131088 | tf_op jit(solution)/shard_map/reduce_scatter | solution.py:38
  322.7 1.0 add_add_fusion
  323.7 1.6 collective-permute-start.1
  325.2 3.5 collective-permute-done.1
  328.7 0.1 copy.14
  328.8 0.7 gather_fusion.2
  329.6 0.1 copy.15
  329.7 0.1 fusion.16
  329.7 35.3 %all_gather.31 = bf16[128,2048]{1,0:T(8,128)(2,1)S(1)} all-gather(bf16[128,256]{1,0:T(8,128)(2,1)S(1)} %fusion.16), channel_id=1, replica_groups=mesh['body'=2,'row'=8,'col'=8] {'row'}, dimensions={1}, use_global_device_ids=true | all-gather | bytes 589824 | tf_op jit(solution)/shard_map/all_gather | solution.py:33
  365.1 7.3 %fusion.28 = f32[128,2048]{1,0:T(8,128)} fusion(bf16[128,2048]{1,0:T(8,128)(2,1)S(1)} %all_gather.31, bf16[2048,2048]{1,0:T(8,128)(2,1)} %bitcast.84), kind=kOutput, calls=%fused_computation.56 | convolution fusion | flops 1073741824 | bytes 9961472 | tf_op jit(solution)/shard_map/dot_general | solution.py:32
  372.4 0.0 reduce-scatter.18.cloned.1.call-update
  372.4 0.0 reduce-scatter.20.cloned.1.call-start
  372.5 31.1 %reduce-scatter.18.cloned.1.call-done = f32[128,256]{1,0:T(8,128)} async-done(((f32[128,2048]{1,0:T(8,128)}), f32[128,256]{1,0:T(8,128)}) %reduce-scatter.18.cloned.1.call-update) | async-done | bytes 131088 | tf_op jit(solution)/shard_map/reduce_scatter | solution.py:38
  403.6 1.0 fusion.20
  404.6 35.5 %all_gather.32 = bf16[128,2048]{1,0:T(8,128)(2,1)S(1)} all-gather(bf16[128,256]{1,0:T(8,128)(2,1)S(1)} %get-tuple-element.11), channel_id=1, replica_groups=mesh['body'=2,'row'=8,'col'=8] {'row'}, dimensions={1}, use_global_device_ids=true | all-gather | bytes 589824 | tf_op jit(solution)/shard_map/all_gather | solution.py:33
  440.1 7.4 %fusion.29 = f32[128,2048]{1,0:T(8,128)} fusion(bf16[128,2048]{1,0:T(8,128)(2,1)S(1)} %all_gather.32, bf16[2048,2048]{1,0:T(8,128)(2,1)} %bitcast.85), kind=kOutput, calls=%fused_computation.57 | convolution fusion | flops 1073741824 | bytes 9961472 | tf_op jit(solution)/shard_map/dot_general | solution.py:32
  447.5 0.0 reduce-scatter.22.cloned.1.call-start
  447.5 30.3 %reduce-scatter.20.cloned.1.call-done = f32[128,256]{1,0:T(8,128)} async-done(((f32[128,2048]{1,0:T(8,128)}), f32[128,256]{1,0:T(8,128)}) %reduce-scatter.20.cloned.1.call-update) | async-done | bytes 131088 | tf_op jit(solution)/shard_map/reduce_scatter | solution.py:38
  477.9 1.0 fusion.13
  478.8 35.8 %all_gather.33 = bf16[128,2048]{1,0:T(8,128)(2,1)S(1)} all-gather(bf16[128,256]{1,0:T(8,128)(2,1)S(1)} %get-tuple-element.9), channel_id=1, replica_groups=mesh['body'=2,'row'=8,'col'=8] {'row'}, dimensions={1}, use_global_device_ids=true | all-gather | bytes 589824 | tf_op jit(solution)/shard_map/all_gather | solution.py:33
  514.6 7.4 %fusion.30 = f32[128,2048]{1,0:T(8,128)} fusion(bf16[128,2048]{1,0:T(8,128)(2,1)S(1)} %all_gather.33, bf16[2048,2048]{1,0:T(8,128)(2,1)} %bitcast.86), kind=kOutput, calls=%fused_computation.58 | convolution fusion | flops 1073741824 | bytes 9961472 | tf_op jit(solution)/shard_map/dot_general | solution.py:32
  522.0 0.0 reduce-scatter.24.cloned.1.call-start
  522.1 30.5 %reduce-scatter.22.cloned.1.call-done = f32[128,256]{1,0:T(8,128)} async-done(((f32[128,2048]{1,0:T(8,128)}), f32[128,256]{1,0:T(8,128)}) %reduce-scatter.22.cloned.1.call-update) | async-done | bytes 131088 | tf_op jit(solution)/shard_map/reduce_scatter | solution.py:38
  552.5 1.0 fusion.18
  553.5 35.5 %all_gather.34 = bf16[128,2048]{1,0:T(8,128)(2,1)S(1)} all-gather(bf16[128,256]{1,0:T(8,128)(2,1)S(1)} %get-tuple-element.6), channel_id=1, replica_groups=mesh['body'=2,'row'=8,'col'=8] {'row'}, dimensions={1}, use_global_device_ids=true | all-gather | bytes 589824 | tf_op jit(solution)/shard_map/all_gather | solution.py:33
  588.9 7.4 %fusion.31 = f32[128,2048]{1,0:T(8,128)} fusion(bf16[128,2048]{1,0:T(8,128)(2,1)S(1)} %all_gather.34, bf16[2048,2048]{1,0:T(8,128)(2,1)} %bitcast.87), kind=kOutput, calls=%fused_computation.59 | convolution fusion | flops 1073741824 | bytes 9961472 | tf_op jit(solution)/shard_map/dot_general | solution.py:32
  596.3 0.0 reduce-scatter.26.cloned.1.call-start
  596.4 30.5 %reduce-scatter.24.cloned.1.call-done = f32[128,256]{1,0:T(8,128)} async-done(((f32[128,2048]{1,0:T(8,128)}), f32[128,256]{1,0:T(8,128)}) %reduce-scatter.24.cloned.1.call-update) | async-done | bytes 131088 | tf_op jit(solution)/shard_map/reduce_scatter | solution.py:38
  626.9 0.9 fusion.9
  627.8 35.4 %all_gather.35 = bf16[128,2048]{1,0:T(8,128)(2,1)S(1)} all-gather(bf16[128,256]{1,0:T(8,128)(2,1)S(1)} %get-tuple-element.4), channel_id=1, replica_groups=mesh['body'=2,'row'=8,'col'=8] {'row'}, dimensions={1}, use_global_device_ids=true | all-gather | bytes 589824 | tf_op jit(solution)/shard_map/all_gather | solution.py:33
  663.2 7.4 %fusion.32 = f32[128,2048]{1,0:T(8,128)} fusion(bf16[128,2048]{1,0:T(8,128)(2,1)S(1)} %all_gather.35, bf16[2048,2048]{1,0:T(8,128)(2,1)} %bitcast.88), kind=kOutput, calls=%fused_computation.60 | convolution fusion | flops 1073741824 | bytes 9961472 | tf_op jit(solution)/shard_map/dot_general | solution.py:32
  670.6 30.5 %reduce-scatter.26.cloned.1.call-done = f32[128,256]{1,0:T(8,128)} async-done(((f32[128,2048]{1,0:T(8,128)}), f32[128,256]{1,0:T(8,128)}) %reduce-scatter.26.cloned.1.call-update) | async-done | bytes 131088 | tf_op jit(solution)/shard_map/reduce_scatter | solution.py:38
  701.1 1.7 subtract_bitcast_fusion
  (22 shorter events, 0.1 us)
Async XLA Ops:
  7.2 2.6 copy-start
  7.2 92.7 %reduce-scatter.10.cloned.1.call-start = ((), (), s32[]{:S(2)}) async-start(), calls=%async_computation.9 | async-start | bytes 1179648 | tf_op jit(solution)/shard_map/reduce_scatter | solution.py:38
  7.2 14.8 %collective-permute-start = (f32[128,256]{1,0:T(8,128)}, f32[128,256]{1,0:T(8,128)S(1)}, u32[]{:S(2)}, u32[]{:S(2)}) collective-permute-start(f32[128,256]{1,0:T(8,128)} %bitcast.90), channel_id=1, source_target_pairs={{0,64},{64,0},{1,65},{65,1},{2,66},{66,2},{3,67},{67,3},{4,68},{68... | collective-permute-start | bytes 393224 | tf_op jit(solution)/shard_map/ppermute | solution.py:12
  11.7 11.3 %copy-start.2 = (f32[1,128,256]{2,1,0:T(8,128)S(1)}, f32[1,128,256]{2,1,0:T(8,128)}, u32[]{:S(2)}) copy-start(f32[1,128,256]{2,1,0:T(8,128)} %param.10) | copy-start | bytes 393220
  22.0 43.7 %copy-start.5 = (s32[1,2]{1,0:T(1,128)S(1)}, s32[1,2]{1,0:T(1,128)}, u32[]{:S(2)}) copy-start(s32[1,2]{1,0:T(1,128)} %param.15) | copy-start | bytes 28
  22.0 77.8 %copy-start.1 = (f32[1,128,256]{2,1,0:T(8,128)S(1)}, f32[1,128,256]{2,1,0:T(8,128)}, u32[]{:S(2)}) copy-start(f32[1,128,256]{2,1,0:T(8,128)} %param.11) | copy-start | bytes 393220
  65.7 108.4 %reduce-scatter.12.cloned.1.call-start = ((), (), s32[]{:S(2)}) async-start(), calls=%async_computation.10 | async-start | bytes 1179648 | tf_op jit(solution)/shard_map/reduce_scatter | solution.py:38
  99.9 74.2 %copy-start.3 = (f32[128,256]{1,0:T(8,128)S(1)}, f32[128,256]{1,0:T(8,128)}, u32[]{:S(2)}) copy-start(f32[128,256]{1,0:T(8,128)} %reduce-scatter.10.cloned.1.call-done) | copy-start | bytes 393220
  143.7 104.7 %reduce-scatter.14.cloned.1.call-start = ((), (), s32[]{:S(2)}) async-start(), calls=%async_computation.11 | async-start | bytes 1179648 | tf_op jit(solution)/shard_map/reduce_scatter | solution.py:38
  218.1 104.6 %reduce-scatter.16.cloned.1.call-start = ((), (), s32[]{:S(2)}) async-start(), calls=%async_computation.12 | async-start | bytes 1179648 | tf_op jit(solution)/shard_map/reduce_scatter | solution.py:38
  292.3 111.3 %reduce-scatter.18.cloned.1.call-start = ((), (), s32[]{:S(2)}) async-start(), calls=%async_computation.13 | async-start | bytes 1179648 | tf_op jit(solution)/shard_map/reduce_scatter | solution.py:38
  323.7 5.0 collective-permute-start.1
  372.4 105.5 %reduce-scatter.20.cloned.1.call-start = ((), (), s32[]{:S(2)}) async-start(), calls=%async_computation.14 | async-start | bytes 1179648 | tf_op jit(solution)/shard_map/reduce_scatter | solution.py:38
  403.6 74.3 %copy-start.4 = (f32[128,256]{1,0:T(8,128)S(1)}, f32[128,256]{1,0:T(8,128)}, u32[]{:S(2)}) copy-start(f32[128,256]{1,0:T(8,128)} %reduce-scatter.18.cloned.1.call-done) | copy-start | bytes 393220
  447.5 105.0 %reduce-scatter.22.cloned.1.call-start = ((), (), s32[]{:S(2)}) async-start(), calls=%async_computation.15 | async-start | bytes 1179648 | tf_op jit(solution)/shard_map/reduce_scatter | solution.py:38
  522.0 104.9 %reduce-scatter.24.cloned.1.call-start = ((), (), s32[]{:S(2)}) async-start(), calls=%async_computation.16 | async-start | bytes 1179648 | tf_op jit(solution)/shard_map/reduce_scatter | solution.py:38
  596.3 104.8 %reduce-scatter.26.cloned.1.call-start = ((), (), s32[]{:S(2)}) async-start(), calls=%async_computation.17 | async-start | bytes 1179648 | tf_op jit(solution)/shard_map/reduce_scatter | solution.py:38
Sparse Core Ops, SparseCore 0:
  65.9 33.9 reduce-scatter.9
  143.8 30.2 reduce-scatter.11
  218.2 30.2 reduce-scatter.13
  292.4 30.2 reduce-scatter.15
  372.6 31.0 reduce-scatter.17
  447.6 30.2 reduce-scatter.19
  522.1 30.3 reduce-scatter.21
  596.4 30.3 reduce-scatter.23
  670.7 30.3 reduce-scatter.25
where the time goes:
time: 710 us; the launch traced here: 709 us
  blocking collectives  319 us (45%)
  waiting for transfers between devices  279 us (39%)
  matrix products  66.2 us (9%)
  between operations  15.7 us (2%)
  local copies, waits for them, and re-layouts  14.7 us (2%)
  other arithmetic  10.3 us (1%)
    all_gather x9, blocking collectives, apply_tile(): lax.all_gather(rounded, 'row', axis=1, tiled=True)  319 us
    reduce_scatter x9, waiting for transfers between devices, apply_tile(): return lax.psum_scatter(partial_sum, 'col', scatter_dimension=1, tiled=True)  276 us
    dot_general x9, matrix products, apply_tile(): lax.dot_general(lax.all_gather(rounded, 'row', axis=1, tiled=True), tile,...  66.2 us
  transfers between devices with their start and end apart: 11, of which 10 were waited for; matrix products, arithmetic and copies ran while one was open for 2% of the time, Pallas kernels for 0%

commit v1 on v0

--- a/solution.py
+++ b/solution.py
@@ -30,7 +30,9 @@
 def apply_tile(field, tile):
     rounded = field.astype(jnp.bfloat16)
     partial_sum = lax.dot_general(
-        lax.all_gather(rounded, "row", axis=1, tiled=True),
+        jnp.concatenate(
+            lax.all_to_all(jnp.stack([rounded] * lax.axis_size("row")), "row", 0, 0), axis=1
+        ),
         tile,
         (((1,), (1,)), ((), ())),
         preferred_element_type=jnp.float32,

time: 710 us -> 526 us (0.74)
  blocking collectives: 319 us -> 134 us
  waiting for transfers between devices: 279 us -> 269 us
    all_gather x9 -> x0, blocking collectives: 319 us -> none  [apply_tile(): lax.all_gather(rounded, 'row', axis=1, tiled=True)]
    all_to_all x0 -> x8, blocking collectives: none -> 134 us  [apply_tile(): lax.all_to_all(jnp.stack([rounded] * lax.axis_size('row')), 'row', 0, 0)]
    reduce_scatter x9, waiting for transfers between devices: 276 us -> 264 us  [apply_tile(): return lax.psum_scatter(partial_sum, 'col', scatter_dimension=1, tiled=True)]
  transfers between devices with their start and end apart: 11 -> 12, of which waited for: 10 -> 12; matrix products, arithmetic and copies ran while one was open for 2% -> 3% of each run, Pallas kernels for 0% -> 0%
where the time goes in v1:
time: 526 us; the launch traced here: 524 us
  waiting for transfers between devices  269 us (51%)
  blocking collectives  134 us (25%)
  matrix products  66.6 us (13%)
  local copies, waits for them, and re-layouts  17.2 us (3%)
  between operations  15.8 us (3%)
  other arithmetic  11.2 us (2%)
  starting transfers between devices  10.7 us (2%)
    reduce_scatter x9, waiting for transfers between devices, apply_tile(): return lax.psum_scatter(partial_sum, 'col', scatter_dimension=1, tiled=True)  264 us
    all_to_all x8, blocking collectives, apply_tile(): lax.all_to_all(jnp.stack([rounded] * lax.axis_size('row')), 'row', 0, 0)  134 us
    dot_general x9, matrix products, apply_tile(): lax.dot_general(jnp.concatenate(lax.all_to_all(jnp.stack([rounded] * lax....  66.6 us
  transfers between devices with their start and end apart: 12, of which 12 were waited for; matrix products, arithmetic and copies ran while one was open for 3% of the time, Pallas kernels for 0%

profile of v1, /device:TPU:0, one launch (start us, length us, event | category | flops | bytes accessed | tf_op | source)
XLA Modules:
  0.0 524.5 jit_solution(518387025785355464)
XLA Ops:
  7.2 1.8 collective-permute-start
  8.9 0.7 compare_and_fusion
  9.7 1.9 gather_fusion.1
  11.7 1.0 collective-permute-done
  12.7 0.1 copy.12
  12.8 0.7 gather_fusion
  13.5 0.1 copy.13
  13.6 1.0 fusion.17
  14.6 0.1 copy.14
  14.7 0.9 stack.18
  15.6 7.1 %all-to-all-start = ((bf16[8,128,256]{1,2,0:T(8,128)(2,1)}), bf16[8,128,256]{1,2,0:T(8,128)(2,1)S(1)}, u32[]{:S(2)}, u32[]{:S(2)}) async-start(bf16[8,128,256]{1,2,0:T(8,128)(2,1)} %stack.18), calls=%async_computation | async-start | bytes 1048576 | tf_op jit(solution)/shard_map/all_to_all | solution.py:34
  22.7 10.3 %copy.25 = bf16[256,8,8,256]{3,1,2,0:T(8,128)(2,1)} copy(bf16[256,8,8,256]{3,2,1,0:T(8,128)(2,1)} %bitcast.116) | data formatting | bytes 16777216
  33.0 0.4 all-to-all-done
  33.4 7.4 %fusion.24 = f32[128,2048]{1,0:T(8,128)} fusion(bf16[128,2048]{0,1:T(8,128)(2,1)S(1)} %bitcast.117, bf16[2048,2048]{1,0:T(8,128)(2,1)} %bitcast.107), kind=kOutput, calls=%fused_computation.52 | convolution fusion | flops 1073741824 | bytes 9961472 | tf_op jit(solution)/shard_map/dot_general | solution.py:32
  40.9 0.6 fusion.23
  42.8 32.9 %reduce-scatter.10.cloned.1.call-done = f32[128,256]{1,0:T(8,128)} async-done(((f32[128,2048]{1,0:T(8,128)}), f32[128,256]{1,0:T(8,128)}) %reduce-scatter.10.cloned.1.call-update) | async-done | bytes 131088 | tf_op jit(solution)/shard_map/reduce_scatter | solution.py:40
  75.7 1.0 fusion.22
  76.7 0.1 copy.15
  76.8 0.1 stack.19
  76.9 16.8 %all_to_all.45 = bf16[8,128,256]{1,2,0:T(8,128)(2,1)S(1)} all-to-all(bf16[8,128,256]{1,2,0:T(8,128)(2,1)S(1)} %stack.19), channel_id=1, replica_groups=mesh['body'=2,'row'=8,'col'=8] {'row'}, dimensions={0} | all-to-all | bytes 1048576 | tf_op jit(solution)/shard_map/all_to_all | solution.py:34
  93.7 7.4 %fusion.25 = f32[128,2048]{1,0:T(8,128)} fusion(bf16[128,2048]{0,1:T(8,128)(2,1)S(1)} %bitcast.119, bf16[2048,2048]{1,0:T(8,128)(2,1)} %bitcast.108), kind=kOutput, calls=%fused_computation.53 | convolution fusion | flops 1073741824 | bytes 9961472 | tf_op jit(solution)/shard_map/dot_general | solution.py:32
  101.3 28.7 %reduce-scatter.12.cloned.1.call-done = f32[128,256]{1,0:T(8,128)} async-done(((f32[128,2048]{1,0:T(8,128)}), f32[128,256]{1,0:T(8,128)}) %reduce-scatter.12.cloned.1.call-update) | async-done | bytes 131088 | tf_op jit(solution)/shard_map/reduce_scatter | solution.py:40
  130.0 1.0 fusion.12
  131.0 0.1 copy.16
  131.1 16.8 %all_to_all.46 = bf16[8,128,256]{1,2,0:T(8,128)(2,1)S(1)} all-to-all(bf16[8,128,256]{1,2,0:T(8,128)(2,1)S(1)} %stack.20), channel_id=1, replica_groups=mesh['body'=2,'row'=8,'col'=8] {'row'}, dimensions={0} | all-to-all | bytes 1048576 | tf_op jit(solution)/shard_map/all_to_all | solution.py:34
  147.9 7.4 %fusion.26 = f32[128,2048]{1,0:T(8,128)} fusion(bf16[128,2048]{0,1:T(8,128)(2,1)S(1)} %bitcast.120, bf16[2048,2048]{1,0:T(8,128)(2,1)} %bitcast.109), kind=kOutput, calls=%fused_computation.54 | convolution fusion | flops 1073741824 | bytes 9961472 | tf_op jit(solution)/shard_map/dot_general | solution.py:32
  155.5 28.8 %reduce-scatter.14.cloned.1.call-done = f32[128,256]{1,0:T(8,128)} async-done(((f32[128,2048]{1,0:T(8,128)}), f32[128,256]{1,0:T(8,128)}) %reduce-scatter.14.cloned.1.call-update) | async-done | bytes 131088 | tf_op jit(solution)/shard_map/reduce_scatter | solution.py:40
  184.3 1.0 fusion.8
  185.2 0.1 copy.17
  185.4 16.7 %all_to_all.47 = bf16[8,128,256]{1,2,0:T(8,128)(2,1)S(1)} all-to-all(bf16[8,128,256]{1,2,0:T(8,128)(2,1)S(1)} %stack.21), channel_id=1, replica_groups=mesh['body'=2,'row'=8,'col'=8] {'row'}, dimensions={0} | all-to-all | bytes 1048576 | tf_op jit(solution)/shard_map/all_to_all | solution.py:34
  202.1 7.4 %fusion.27 = f32[128,2048]{1,0:T(8,128)} fusion(bf16[128,2048]{0,1:T(8,128)(2,1)S(1)} %bitcast.121, bf16[2048,2048]{1,0:T(8,128)(2,1)} %bitcast.110), kind=kOutput, calls=%fused_computation.55 | convolution fusion | flops 1073741824 | bytes 9961472 | tf_op jit(solution)/shard_map/dot_general | solution.py:32
  209.7 28.8 %reduce-scatter.16.cloned.1.call-done = f32[128,256]{1,0:T(8,128)} async-done(((f32[128,2048]{1,0:T(8,128)}), f32[128,256]{1,0:T(8,128)}) %reduce-scatter.16.cloned.1.call-update) | async-done | bytes 131088 | tf_op jit(solution)/shard_map/reduce_scatter | solution.py:40
  238.5 1.0 add_add_fusion
  239.5 1.5 collective-permute-start.1
  241.0 3.6 collective-permute-done.1
  244.6 0.1 copy.18
  244.7 0.7 gather_fusion.2
  245.4 0.1 copy.19
  245.6 0.1 copy.20
  245.7 0.1 stack.22
  245.8 16.7 %all_to_all.48 = bf16[8,128,256]{1,2,0:T(8,128)(2,1)S(1)} all-to-all(bf16[8,128,256]{1,2,0:T(8,128)(2,1)S(1)} %stack.22), channel_id=1, replica_groups=mesh['body'=2,'row'=8,'col'=8] {'row'}, dimensions={0} | all-to-all | bytes 1048576 | tf_op jit(solution)/shard_map/all_to_all | solution.py:34
  262.5 7.4 %fusion.28 = f32[128,2048]{1,0:T(8,128)} fusion(bf16[128,2048]{0,1:T(8,128)(2,1)S(1)} %bitcast.122, bf16[2048,2048]{1,0:T(8,128)(2,1)} %bitcast.111), kind=kOutput, calls=%fused_computation.56 | convolution fusion | flops 1073741824 | bytes 9961472 | tf_op jit(solution)/shard_map/dot_general | solution.py:32
  270.0 29.4 %reduce-scatter.18.cloned.1.call-done = f32[128,256]{1,0:T(8,128)} async-done(((f32[128,2048]{1,0:T(8,128)}), f32[128,256]{1,0:T(8,128)}) %reduce-scatter.18.cloned.1.call-update) | async-done | bytes 131088 | tf_op jit(solution)/shard_map/reduce_scatter | solution.py:40
  299.3 1.0 fusion.20
  300.3 0.1 copy.21
  300.5 16.8 %all_to_all.49 = bf16[8,128,256]{1,2,0:T(8,128)(2,1)S(1)} all-to-all(bf16[8,128,256]{1,2,0:T(8,128)(2,1)S(1)} %stack.23), channel_id=1, replica_groups=mesh['body'=2,'row'=8,'col'=8] {'row'}, dimensions={0} | all-to-all | bytes 1048576 | tf_op jit(solution)/shard_map/all_to_all | solution.py:34
  317.3 7.4 %fusion.29 = f32[128,2048]{1,0:T(8,128)} fusion(bf16[128,2048]{0,1:T(8,128)(2,1)S(1)} %bitcast.123, bf16[2048,2048]{1,0:T(8,128)(2,1)} %bitcast.112), kind=kOutput, calls=%fused_computation.57 | convolution fusion | flops 1073741824 | bytes 9961472 | tf_op jit(solution)/shard_map/dot_general | solution.py:32
  324.8 28.9 %reduce-scatter.20.cloned.1.call-done = f32[128,256]{1,0:T(8,128)} async-done(((f32[128,2048]{1,0:T(8,128)}), f32[128,256]{1,0:T(8,128)}) %reduce-scatter.20.cloned.1.call-update) | async-done | bytes 131088 | tf_op jit(solution)/shard_map/reduce_scatter | solution.py:40
  353.7 1.0 fusion.13
  354.6 0.1 copy.22
  354.8 16.7 %all_to_all.50 = bf16[8,128,256]{1,2,0:T(8,128)(2,1)S(1)} all-to-all(bf16[8,128,256]{1,2,0:T(8,128)(2,1)S(1)} %stack.24), channel_id=1, replica_groups=mesh['body'=2,'row'=8,'col'=8] {'row'}, dimensions={0} | all-to-all | bytes 1048576 | tf_op jit(solution)/shard_map/all_to_all | solution.py:34
  371.5 7.4 %fusion.30 = f32[128,2048]{1,0:T(8,128)} fusion(bf16[128,2048]{0,1:T(8,128)(2,1)S(1)} %bitcast.124, bf16[2048,2048]{1,0:T(8,128)(2,1)} %bitcast.113), kind=kOutput, calls=%fused_computation.58 | convolution fusion | flops 1073741824 | bytes 9961472 | tf_op jit(solution)/shard_map/dot_general | solution.py:32
  379.0 29.0 %reduce-scatter.22.cloned.1.call-done = f32[128,256]{1,0:T(8,128)} async-done(((f32[128,2048]{1,0:T(8,128)}), f32[128,256]{1,0:T(8,128)}) %reduce-scatter.22.cloned.1.call-update) | async-done | bytes 131088 | tf_op jit(solution)/shard_map/reduce_scatter | solution.py:40
  407.9 1.0 fusion.18
  408.9 0.1 copy.23
  409.1 16.7 %all_to_all.51 = bf16[8,128,256]{1,2,0:T(8,128)(2,1)S(1)} all-to-all(bf16[8,128,256]{1,2,0:T(8,128)(2,1)S(1)} %stack.25), channel_id=1, replica_groups=mesh['body'=2,'row'=8,'col'=8] {'row'}, dimensions={0} | all-to-all | bytes 1048576 | tf_op jit(solution)/shard_map/all_to_all | solution.py:34
  425.8 7.4 %fusion.31 = f32[128,2048]{1,0:T(8,128)} fusion(bf16[128,2048]{0,1:T(8,128)(2,1)S(1)} %bitcast.125, bf16[2048,2048]{1,0:T(8,128)(2,1)} %bitcast.114), kind=kOutput, calls=%fused_computation.59 | convolution fusion | flops 1073741824 | bytes 9961472 | tf_op jit(solution)/shard_map/dot_general | solution.py:32
  433.2 28.9 %reduce-scatter.24.cloned.1.call-done = f32[128,256]{1,0:T(8,128)} async-done(((f32[128,2048]{1,0:T(8,128)}), f32[128,256]{1,0:T(8,128)}) %reduce-scatter.24.cloned.1.call-update) | async-done | bytes 131088 | tf_op jit(solution)/shard_map/reduce_scatter | solution.py:40
  462.1 0.9 fusion.9
  463.1 0.1 copy.24
  463.3 16.7 %all_to_all.52 = bf16[8,128,256]{1,2,0:T(8,128)(2,1)S(1)} all-to-all(bf16[8,128,256]{1,2,0:T(8,128)(2,1)S(1)} %stack.26), channel_id=1, replica_groups=mesh['body'=2,'row'=8,'col'=8] {'row'}, dimensions={0} | all-to-all | bytes 1048576 | tf_op jit(solution)/shard_map/all_to_all | solution.py:34
  479.9 7.4 %fusion.32 = f32[128,2048]{1,0:T(8,128)} fusion(bf16[128,2048]{0,1:T(8,128)(2,1)S(1)} %bitcast.118, bf16[2048,2048]{1,0:T(8,128)(2,1)} %bitcast.115), kind=kOutput, calls=%fused_computation.60 | convolution fusion | flops 1073741824 | bytes 9961472 | tf_op jit(solution)/shard_map/dot_general | solution.py:32
  487.4 28.9 %reduce-scatter.26.cloned.1.call-done = f32[128,256]{1,0:T(8,128)} async-done(((f32[128,2048]{1,0:T(8,128)}), f32[128,256]{1,0:T(8,128)}) %reduce-scatter.26.cloned.1.call-update) | async-done | bytes 131088 | tf_op jit(solution)/shard_map/reduce_scatter | solution.py:40
  516.3 1.7 subtract_bitcast_fusion
  (41 shorter events, 1.0 us)
Async XLA Ops:
  7.2 2.5 copy-start
  7.2 5.5 %collective-permute-start = (f32[128,256]{1,0:T(8,128)}, f32[128,256]{1,0:T(8,128)S(1)}, u32[]{:S(2)}, u32[]{:S(2)}) collective-permute-start(f32[128,256]{1,0:T(8,128)} %bitcast.126), channel_id=1, source_target_pairs={{0,64},{64,0},{1,65},{65,1},{2,66},{66,2},{3,67},{67,3},{4,68},{68... | collective-permute-start | bytes 393224 | tf_op jit(solution)/shard_map/ppermute | solution.py:12
  15.6 17.8 %all-to-all-start = ((bf16[8,128,256]{1,2,0:T(8,128)(2,1)}), bf16[8,128,256]{1,2,0:T(8,128)(2,1)S(1)}, u32[]{:S(2)}, u32[]{:S(2)}) async-start(bf16[8,128,256]{1,2,0:T(8,128)(2,1)} %stack.18), calls=%async_computation | async-start | bytes 1048576 | tf_op jit(solution)/shard_map/all_to_all | solution.py:34
  22.7 53.0 %reduce-scatter.10.cloned.1.call-start = ((), (), s32[]{:S(2)}) async-start(), calls=%async_computation.18 | async-start | bytes 1179648 | tf_op jit(solution)/shard_map/reduce_scatter | solution.py:40
  33.0 7.9 %copy-start.5 = (s32[1,2]{1,0:T(1,128)S(1)}, s32[1,2]{1,0:T(1,128)}, u32[]{:S(2)}) copy-start(s32[1,2]{1,0:T(1,128)} %param.15) | copy-start | bytes 28
  33.0 42.7 %copy-start.1 = (f32[1,128,256]{2,1,0:T(8,128)S(1)}, f32[1,128,256]{2,1,0:T(8,128)}, u32[]{:S(2)}) copy-start(f32[1,128,256]{2,1,0:T(8,128)} %param.11) | copy-start | bytes 393220
  40.8 89.2 %reduce-scatter.12.cloned.1.call-start = ((), (), s32[]{:S(2)}) async-start(), calls=%async_computation.19 | async-start | bytes 1179648 | tf_op jit(solution)/shard_map/reduce_scatter | solution.py:40
  75.7 54.3 %copy-start.3 = (f32[128,256]{1,0:T(8,128)S(1)}, f32[128,256]{1,0:T(8,128)}, u32[]{:S(2)}) copy-start(f32[128,256]{1,0:T(8,128)} %reduce-scatter.10.cloned.1.call-done) | copy-start | bytes 393220
  101.1 83.2 %reduce-scatter.14.cloned.1.call-start = ((), (), s32[]{:S(2)}) async-start(), calls=%async_computation.20 | async-start | bytes 1179648 | tf_op jit(solution)/shard_map/reduce_scatter | solution.py:40
  155.3 83.2 %copy-start.2 = (f32[1,128,256]{2,1,0:T(8,128)S(1)}, f32[1,128,256]{2,1,0:T(8,128)}, u32[]{:S(2)}) copy-start(f32[1,128,256]{2,1,0:T(8,128)} %param.10) | copy-start | bytes 393220
  155.3 83.2 %reduce-scatter.16.cloned.1.call-start = ((), (), s32[]{:S(2)}) async-start(), calls=%async_computation.21 | async-start | bytes 1179648 | tf_op jit(solution)/shard_map/reduce_scatter | solution.py:40
  209.5 89.8 %reduce-scatter.18.cloned.1.call-start = ((), (), s32[]{:S(2)}) async-start(), calls=%async_computation.22 | async-start | bytes 1179648 | tf_op jit(solution)/shard_map/reduce_scatter | solution.py:40
  239.5 5.0 collective-permute-start.1
  269.9 83.8 %reduce-scatter.20.cloned.1.call-start = ((), (), s32[]{:S(2)}) async-start(), calls=%async_computation.23 | async-start | bytes 1179648 | tf_op jit(solution)/shard_map/reduce_scatter | solution.py:40
  299.3 54.3 %copy-start.4 = (f32[128,256]{1,0:T(8,128)S(1)}, f32[128,256]{1,0:T(8,128)}, u32[]{:S(2)}) copy-start(f32[128,256]{1,0:T(8,128)} %reduce-scatter.18.cloned.1.call-done) | copy-start | bytes 393220
  324.8 83.2 %reduce-scatter.22.cloned.1.call-start = ((), (), s32[]{:S(2)}) async-start(), calls=%async_computation.24 | async-start | bytes 1179648 | tf_op jit(solution)/shard_map/reduce_scatter | solution.py:40
  378.9 83.2 %reduce-scatter.24.cloned.1.call-start = ((), (), s32[]{:S(2)}) async-start(), calls=%async_computation.25 | async-start | bytes 1179648 | tf_op jit(solution)/shard_map/reduce_scatter | solution.py:40
  433.2 83.1 %reduce-scatter.26.cloned.1.call-start = ((), (), s32[]{:S(2)}) async-start(), calls=%async_computation.26 | async-start | bytes 1179648 | tf_op jit(solution)/shard_map/reduce_scatter | solution.py:40
Sparse Core Ops, SparseCore 0:
  41.0 34.6 reduce-scatter.9
  101.2 28.7 reduce-scatter.11
  155.5 28.7 reduce-scatter.13
  209.7 28.8 reduce-scatter.15
  270.0 29.2 reduce-scatter.17
  324.9 28.7 reduce-scatter.19
  379.0 28.8 reduce-scatter.21
  433.3 28.7 reduce-scatter.23
  487.5 28.7 reduce-scatter.25
